TPU v7x, 256 devices: a whole 4x4x8 slice. The times are simulated.
256 devices in a mesh: ew: 8 (over y, z_hi), ns: 32 (over z_lo, x, core).
Axes of the slice: x: 4, y: 4, z: 8 (z_hi: 2, z_lo: 4; z = z_hi * 4 + z_lo), core: 2. Of those that a mesh axis runs over, the one named last changes fastest.
Arguments:
- couplings: bfloat16 [8, 32, 16, 128, 2048], P('ew', 'ns'), may hold values from -0.125 to 0.125
- inverses: bfloat16 [8, 32, 16, 128, 128], P('ew', 'ns'), as said below
- pattern: int32 [8, 32, 16, 16], P('ew', 'ns'), may hold values 0 or 1
- counts: int32 [8, 32], P('ew', 'ns'), may hold values from 1 to 16, as said below
- basis: bfloat16 [8, 32, 128, 2048], P('ew', 'ns'), may hold values from -0.125 to 0.125
Outputs:
- south_front: float32 [8, 32, 768, 768], P('ew', 'ns')
- west_front: float32 [8, 32, 256, 256], P('ew', 'ns')
- coarse: float32 [8, 32, 128, 128], P('ew', 'ns')
Inputs may be any that keep to these rules, and one draw needn't show every extreme that they name: `counts`: some subdomain has exactly 16 live block columns. `inverses`: each block is symmetric.
All inputs are finite; a program needn't handle non-finite values. No bound on the sum of `pattern` on one device may be relied on, other than what follows from the above.
Results may differ from a plain program's by a relative error of at most 0.0015.
Values may be sent and summed in bfloat16 or wider, within the bound.
No kernel may reach another device: no remote copies, remote signals or barrier semaphores. Data moves between devices by JAX's collectives and lax.ppermute only.
A program may use at most 128 MiB of HBM per device.

v0:
```python
import jax
import jax.numpy as jnp
from jax import lax
from jax.sharding import PartitionSpec as P

B = 128
SN = 6
SE = 2


def from_behind(block, axis, distance):
    devices = range(lax.axis_size(axis))
    route = [(i - distance, i) for i in devices if i - distance in devices]
    return lax.ppermute(block, axis, route)


def solve_all(slabs, inverse):
    return jnp.einsum("kab,kbc->kac", inverse, slabs, preferred_element_type=jnp.float32).astype(
        jnp.bfloat16
    )


def edge_parts(slabs, solved, edges):
    results = []
    for edge in edges:
        slab = slabs[:, :, edge[0] : edge[0] + edge[1]]
        answer = solved[:, :, edge[0] : edge[0] + edge[1]]
        results.append(-jnp.einsum("kbi,kbj->ij", slab, answer, preferred_element_type=jnp.float32))
    return tuple(results)


def pass_edges(high_parts):
    from_west = from_behind(high_parts[0], "ew", 1)
    from_south = from_behind(high_parts[1], "ns", 1)
    return (from_west, from_south)


def shards(couplings, inverses, pattern, counts, basis):
    coupling = couplings[0, 0]
    inverse = inverses[0, 0]
    touched = pattern[0, 0]
    count = counts[0, 0]
    blocks_total = coupling.shape[0]
    north_start = SN * B
    west_start = 2 * SN * B
    east_start = west_start + SE * B
    south_edge = (0, SN * B)
    north_edge = (north_start, SN * B)
    west_edge = (west_start, SE * B)
    east_edge = (east_start, SE * B)
    columns = jnp.repeat(touched, B, axis=1)
    live = (jnp.arange(blocks_total, dtype=jnp.int32) < count).astype(jnp.int32)[:, None]
    keep = (columns * live).astype(jnp.bfloat16)
    masked = coupling * keep[:, None, :]
    high_edges = [east_edge, north_edge]
    solved = solve_all(masked, inverse)
    every_part = edge_parts(masked, solved, [south_edge, west_edge] + high_edges)
    low_parts = every_part[:2]
    from_west, from_south = pass_edges(every_part[2:])
    south_front = low_parts[0] + from_south
    west_front = low_parts[1] + from_west
    front_half = west_front.astype(jnp.bfloat16)
    row_basis = basis[0, 0]
    rank = row_basis.shape[0]
    edge_width = SE * B
    piece = lax.all_gather(front_half, "ew", axis=0, tiled=True)
    pieces = piece.shape[0] // edge_width
    columns_here = row_basis.reshape(rank, pieces, edge_width)
    fronts = piece.reshape(pieces, edge_width, edge_width)
    projected = jnp.einsum(
        "rnk,nkl->rnl", columns_here, fronts, preferred_element_type=jnp.float32
    ).astype(jnp.bfloat16)
    coarse = jnp.einsum("rnl,snl->rs", projected, columns_here, preferred_element_type=jnp.float32)
    return (south_front[None, None], west_front[None, None], coarse[None, None])


def solution(mesh):
    return jax.shard_map(
        shards,
        mesh=mesh,
        in_specs=(
            P("ew", "ns", None, None, None),
            P("ew", "ns", None, None, None),
            P("ew", "ns", None, None),
            P("ew", "ns"),
            P("ew", "ns", None, None),
        ),
        out_specs=(P("ew", "ns", None, None), P("ew", "ns", None, None), P("ew", "ns", None, None)),
        check_vma=False,
    )
```

profile of v0, /device:TPU:2, one launch (start us, length us, event | category | flops | bytes accessed | tf_op | source)
XLA Modules:
  0.0 137.7 jit_solution(6369991985110612012)
XLA Ops:
  7.2 0.0 copy-start
  7.2 0.0 copy-start.3
  7.2 0.0 all-gather.2.cloned.1.call-start
  7.2 12.3 %copy.8 = bf16[1,1,16,128,2048]{3,4,2,1,0:T(8,128)(2,1)} copy(bf16[1,1,16,128,2048]{4,3,2,1,0:T(8,128)(2,1)} %param.5) | data formatting | bytes 16777216 | tf_op args[0]
  20.2 0.0 copy-done.3
  20.3 0.1 broadcast_in_dim.14
  20.4 0.1 fusion.29
  20.4 6.4 %bitcast_multiply_fusion = bf16[16,128,2048]{1,2,0:T(8,128)(2,1)S(1)} fusion(bf16[1,1,16,128,2048]{3,4,2,1,0:T(8,128)(2,1)} %copy.8, bf16[16,2048]{1,0:T(8,128)(2,1)S(1)} %fusion.29), kind=kLoop, calls=%fused_computation | loop fusion | flops 4194304 | bytes 16842752 | tf_op jit(solution)/shard_map/mul | solution.py:54
  26.8 0.0 copy-done
  26.8 0.0 copy-start.1
  26.8 5.1 %convert_bitcast_fusion = bf16[16,128,2048]{1,2,0:T(8,128)(2,1)} fusion(bf16[16,128,2048]{1,2,0:T(8,128)(2,1)S(1)} %bitcast_multiply_fusion, bf16[1,1,16,128,128]{4,3,2,1,0:T(8,128)(2,1)S(1)} %copy-done), kind=kOutput, calls=%fused_computation.1 | convolution fusion | flops 1077936128 | bytes 17301504 | tf_op jit(solution)/shard_map/kab,kbc->kac/dot_general | solution.py:18
  31.9 2.0 %fusion.18 = f32[256,256]{1,0:T(8,128)S(1)} fusion(bf16[16,128,2048]{1,2,0:T(8,128)(2,1)} %convert_bitcast_fusion, bf16[16,128,2048]{1,2,0:T(8,128)(2,1)S(1)} %bitcast_multiply_fusion), kind=kOutput, calls=%fused_computation.16 | convolution fusion | flops 268500992 | bytes 2359296 | tf_op jit(solution)/shard_map/kbi,kbj->ij/dot_general | solution.py:28
  33.9 0.0 copy-start.2
  33.9 9.2 %collective-permute-start.1 = (f32[256,256]{1,0:T(8,128)S(1)}, f32[256,256]{1,0:T(8,128)S(1)}, u32[]{:S(2)}, u32[]{:S(2)}) collective-permute-start(f32[256,256]{1,0:T(8,128)S(1)} %fusion.18), channel_id=1, source_target_pairs={{0,32},{32,64},{64,96},{96,128},{128,160},{160,192},{192,224},{1,3... | collective-permute-start | bytes 786440 | tf_op jit(solution)/shard_map/ppermute | solution.py:14
  43.1 5.9 %bitcast_negate_fusion = f32[768,768]{1,0:T(8,128)} fusion(bf16[16,128,2048]{1,2,0:T(8,128)(2,1)} %convert_bitcast_fusion, bf16[16,128,2048]{1,2,0:T(8,128)(2,1)S(1)} %bitcast_multiply_fusion), kind=kOutput, calls=%fused_computation.8 | convolution fusion | flops 2416508928 | bytes 8650752 | tf_op jit(solution)/shard_map/kbi,kbj->ij/dot_general | solution.py:28
  49.1 1.9 %collective-permute-start = (f32[768,768]{1,0:T(8,128)}, f32[768,768]{1,0:T(8,128)}, u32[]{:S(2)}, u32[]{:S(2)}) collective-permute-start(f32[768,768]{1,0:T(8,128)} %bitcast_negate_fusion), channel_id=1, source_target_pairs={{0,1},{1,2},{2,3},{3,4},{4,5},{5,6},{6,7},{7,8},{8,9},{9,10},{10,1... | collective-permute-start | bytes 7077896 | tf_op jit(solution)/shard_map/ppermute | solution.py:14
  51.0 0.0 collective-permute-done.1
  51.0 0.0 copy-done.1
  51.0 2.4 %fusion.30 = (bf16[256,256]{1,0:T(8,128)(2,1)}, f32[256,256]{1,0:T(8,128)}) fusion(f32[256,256]{1,0:T(8,128)S(1)} %collective-permute-done.1, bf16[16,128,2048]{1,2,0:T(8,128)(2,1)} %convert_bitcast_fusion, bf16[16,128,2048]{1,2,0:T(8,128)(2,1)S(1)} %bitcast_multiply_fusion), kind=kOutput, calls=%fused_computation.30 | convolution fusion | flops 268632064 | bytes 2752512 | tf_op jit(solution)/shard_map/kbi,kbj->ij/dot_general | solution.py:28
  53.5 0.0 all-gather.2.cloned.1.call-update
  53.5 0.0 copy-done.2
  53.5 0.1 copy.20
  53.6 67.2 %all-gather.2.cloned.1.call-done = bf16[2048,256]{1,0:T(8,128)(2,1)} async-done(((bf16[256,256]{1,0:T(8,128)(2,1)}), bf16[2048,256]{1,0:T(8,128)(2,1)}) %all-gather.2.cloned.1.call-update) | async-done | bytes 1048592 | tf_op jit(solution)/shard_map/all_gather | solution.py:66
  120.8 2.4 %fusion.21 = f32[1,1,128,128]{3,2,1,0:T(8,128)} fusion(bf16[8,256,256]{2,1,0:T(8,128)(2,1)} %bitcast.57, bf16[128,8,256]{2,1,0:T(8,128)(2,1)S(1)} %bitcast.54), kind=kOutput, calls=%fused_computation.20 | convolution fusion | flops 201588736 | bytes 1638400 | tf_op jit(solution)/shard_map/rnl,snl->rs/dot_general | solution.py:73
  123.2 0.0 collective-permute-done
  123.2 7.6 %fusion.7 = f32[1,1,768,768]{3,2,1,0:T(8,128)} fusion(f32[768,768]{1,0:T(8,128)} %collective-permute-done, bf16[16,128,2048]{1,2,0:T(8,128)(2,1)} %convert_bitcast_fusion, bf16[16,128,2048]{1,2,0:T(8,128)(2,1)} %copy-done.1), kind=kOutput, calls=%fused_computation.11 | convolution fusion | flops 2417098752 | bytes 11010048 | tf_op jit(solution)/shard_map/kbi,kbj->ij/dot_general | solution.py:28
  (1 shorter events, 0.0 us)
Async XLA Ops:
  7.2 19.7 %copy-start = (bf16[1,1,16,128,128]{4,3,2,1,0:T(8,128)(2,1)S(1)}, bf16[1,1,16,128,128]{4,3,2,1,0:T(8,128)(2,1)}, u32[]{:S(2)}) copy-start(bf16[1,1,16,128,128]{4,3,2,1,0:T(8,128)(2,1)} %param.6) | copy-start | bytes 1572868
  7.2 13.1 %copy-start.3 = (s32[1,1,16,16]{3,2,1,0:T(8,128)S(1)}, s32[1,1,16,16]{3,2,1,0:T(8,128)}, u32[]{:S(2)}) copy-start(s32[1,1,16,16]{3,2,1,0:T(8,128)} %param.7) | copy-start | bytes 3076
  7.2 113.6 %all-gather.2.cloned.1.call-start = ((), (), s32[]{:S(2)}) async-start(), calls=%async_computation | async-start | bytes 1179648 | tf_op jit(solution)/shard_map/all_gather | solution.py:66
  26.8 24.2 %copy-start.1 = (bf16[16,128,2048]{1,2,0:T(8,128)(2,1)}, bf16[16,128,2048]{1,2,0:T(8,128)(2,1)S(1)}, u32[]{:S(2)}) copy-start(bf16[16,128,2048]{1,2,0:T(8,128)(2,1)S(1)} %bitcast_multiply_fusion) | copy-start | bytes 25165828
  33.9 19.6 %copy-start.2 = (bf16[1,1,128,2048]{3,2,1,0:T(8,128)(2,1)S(1)}, bf16[1,1,128,2048]{3,2,1,0:T(8,128)(2,1)}, u32[]{:S(2)}) copy-start(bf16[1,1,128,2048]{3,2,1,0:T(8,128)(2,1)} %param.9) | copy-start | bytes 1572868
  33.9 17.1 %collective-permute-start.1 = (f32[256,256]{1,0:T(8,128)S(1)}, f32[256,256]{1,0:T(8,128)S(1)}, u32[]{:S(2)}, u32[]{:S(2)}) collective-permute-start(f32[256,256]{1,0:T(8,128)S(1)} %fusion.18), channel_id=1, source_target_pairs={{0,32},{32,64},{64,96},{96,128},{128,160},{160,192},{192,224},{1,3... | collective-permute-start | bytes 786440 | tf_op jit(solution)/shard_map/ppermute | solution.py:14
  49.1 74.1 %collective-permute-start = (f32[768,768]{1,0:T(8,128)}, f32[768,768]{1,0:T(8,128)}, u32[]{:S(2)}, u32[]{:S(2)}) collective-permute-start(f32[768,768]{1,0:T(8,128)} %bitcast_negate_fusion), channel_id=1, source_target_pairs={{0,1},{1,2},{2,3},{3,4},{4,5},{5,6},{6,7},{7,8},{8,9},{9,10},{10,1... | collective-permute-start | bytes 7077896 | tf_op jit(solution)/shard_map/ppermute | solution.py:14
Sparse Core Ops, SparseCore 0:
  53.6 67.1 all-gather.1
where the time goes:
time: 138 us
  waiting for transfers between devices  67.2 us (49%)
  matrix products  25.4 us (18%)
  between operations  14.8 us (11%)
  local copies, waits for them, and re-layouts  12.6 us (9%)
  starting transfers between devices  11.2 us (8%)
  other arithmetic  6.46 us (5%)
    all_gather x1, waiting for transfers between devices, shards(): piece = lax.all_gather(front_half, 'ew', axis=0, tiled=True)  67.2 us
    dot_general x4, matrix products, edge_parts(): jnp.einsum('kbi,kbj->ij', slab, answer, preferred_element_type=jnp.float32)  17.9 us
    unnamed x10, local copies, waits for them, and re-layouts  12.5 us
    ppermute x2, starting transfers between devices, from_behind(): return lax.ppermute(block, axis, route)  11.2 us
    mul x1, other arithmetic, shards(): masked = coupling * keep[:, None, :]  6.38 us
    dot_general x1, matrix products, solve_all(): jnp.einsum('kab,kbc->kac', inverse, slabs, preferred_element_type=jnp.flo...  5.05 us
  transfers between devices with their start and end apart: 3, of which 1 were waited for; matrix products, arithmetic and copies ran while one was open for 8% of the time, Pallas kernels for 0%

commit v1 on v0

--- a/solution.py
+++ b/solution.py
@@ -63,7 +63,8 @@
     row_basis = basis[0, 0]
     rank = row_basis.shape[0]
     edge_width = SE * B
-    piece = lax.all_gather(front_half, "ew", axis=0, tiled=True)
+    sent = jnp.stack([front_half] * lax.axis_size("ew"))
+    piece = jnp.concatenate(lax.all_to_all(sent, "ew", 0, 0), axis=0)
     pieces = piece.shape[0] // edge_width
     columns_here = row_basis.reshape(rank, pieces, edge_width)
     fronts = piece.reshape(pieces, edge_width, edge_width)

time: 138 us -> 109 us (0.79)
  the two profiles are of different devices: /device:TPU:2 before, /device:TPU:7 now
where the time goes in v1:
time: 109 us
  waiting for transfers between devices  44 us (40%)
  matrix products  24.1 us (22%)
  starting transfers between devices  19.2 us (18%)
  local copies, waits for them, and re-layouts  13.7 us (13%)
  other arithmetic  6.46 us (6%)
  between operations  1.41 us (1%)
    all_to_all x1, waiting for transfers between devices, shards(): piece = jnp.concatenate(lax.all_to_all(sent, 'ew', 0, 0), axis=0)  44 us
    dot_general x4, matrix products, edge_parts(): jnp.einsum('kbi,kbj->ij', slab, answer, preferred_element_type=jnp.float32)  17.9 us
    unnamed x10, local copies, waits for them, and re-layouts  12.5 us
    ppermute x2, starting transfers between devices, from_behind(): return lax.ppermute(block, axis, route)  12.3 us
    all_to_all x1, starting transfers between devices, shards(): piece = jnp.concatenate(lax.all_to_all(sent, 'ew', 0, 0), axis=0)  6.8 us
    mul x1, other arithmetic, shards(): masked = coupling * keep[:, None, :]  6.38 us
    dot_general x1, matrix products, solve_all(): jnp.einsum('kab,kbc->kac', inverse, slabs, preferred_element_type=jnp.flo...  5.06 us
  transfers between devices with their start and end apart: 3, of which 1 were waited for; matrix products, arithmetic and copies ran while one was open for 10% of the time, Pallas kernels for 0%

profile of v1, /device:TPU:7, one launch (start us, length us, event | category | flops | bytes accessed | tf_op | source)
XLA Modules:
  0.0 108.8 jit_solution(7335699066726274290)
XLA Ops:
  0.6 0.0 copy-start
  0.6 0.0 copy-start.3
  0.7 12.4 %copy.8 = bf16[1,1,16,128,2048]{3,4,2,1,0:T(8,128)(2,1)} copy(bf16[1,1,16,128,2048]{4,3,2,1,0:T(8,128)(2,1)} %param.5) | data formatting | bytes 16777216 | tf_op args[0]
  13.7 0.0 copy-done.3
  13.7 0.1 broadcast_in_dim.14
  13.8 0.1 fusion.29
  13.9 6.4 %bitcast_multiply_fusion = bf16[16,128,2048]{1,2,0:T(8,128)(2,1)S(1)} fusion(bf16[1,1,16,128,2048]{3,4,2,1,0:T(8,128)(2,1)} %copy.8, bf16[16,2048]{1,0:T(8,128)(2,1)S(1)} %fusion.29), kind=kLoop, calls=%fused_computation | loop fusion | flops 4194304 | bytes 16842752 | tf_op jit(solution)/shard_map/mul | solution.py:54
  20.3 0.0 copy-done
  20.3 0.0 copy-start.1
  20.3 5.1 %convert_bitcast_fusion = bf16[16,128,2048]{1,2,0:T(8,128)(2,1)} fusion(bf16[16,128,2048]{1,2,0:T(8,128)(2,1)S(1)} %bitcast_multiply_fusion, bf16[1,1,16,128,128]{4,3,2,1,0:T(8,128)(2,1)S(1)} %copy-done), kind=kOutput, calls=%fused_computation.1 | convolution fusion | flops 1077936128 | bytes 17301504 | tf_op jit(solution)/shard_map/kab,kbc->kac/dot_general | solution.py:18
  25.4 2.0 %fusion.18 = f32[256,256]{1,0:T(8,128)S(1)} fusion(bf16[16,128,2048]{1,2,0:T(8,128)(2,1)} %convert_bitcast_fusion, bf16[16,128,2048]{1,2,0:T(8,128)(2,1)S(1)} %bitcast_multiply_fusion), kind=kOutput, calls=%fused_computation.16 | convolution fusion | flops 268500992 | bytes 2359296 | tf_op jit(solution)/shard_map/kbi,kbj->ij/dot_general | solution.py:28
  27.3 0.0 copy-start.2
  27.3 9.0 %collective-permute-start.1 = (f32[256,256]{1,0:T(8,128)S(1)}, f32[256,256]{1,0:T(8,128)S(1)}, u32[]{:S(2)}, u32[]{:S(2)}) collective-permute-start(f32[256,256]{1,0:T(8,128)S(1)} %fusion.18), channel_id=1, source_target_pairs={{0,32},{32,64},{64,96},{96,128},{128,160},{160,192},{192,224},{1,3... | collective-permute-start | bytes 786440 | tf_op jit(solution)/shard_map/ppermute | solution.py:14
  36.3 5.9 %bitcast_negate_fusion = f32[768,768]{1,0:T(8,128)} fusion(bf16[16,128,2048]{1,2,0:T(8,128)(2,1)} %convert_bitcast_fusion, bf16[16,128,2048]{1,2,0:T(8,128)(2,1)S(1)} %bitcast_multiply_fusion), kind=kOutput, calls=%fused_computation.8 | convolution fusion | flops 2416508928 | bytes 8650752 | tf_op jit(solution)/shard_map/kbi,kbj->ij/dot_general | solution.py:28
  42.2 3.4 %collective-permute-start = (f32[768,768]{1,0:T(8,128)}, f32[768,768]{1,0:T(8,128)}, u32[]{:S(2)}, u32[]{:S(2)}) collective-permute-start(f32[768,768]{1,0:T(8,128)} %bitcast_negate_fusion), channel_id=1, source_target_pairs={{0,1},{1,2},{2,3},{3,4},{4,5},{5,6},{6,7},{7,8},{8,9},{9,10},{10,1... | collective-permute-start | bytes 7077896 | tf_op jit(solution)/shard_map/ppermute | solution.py:14
  45.6 0.0 collective-permute-done.1
  45.7 0.0 copy-done.1
  45.7 2.4 %fusion.30 = (bf16[256,256]{1,0:T(8,128)(2,1)S(1)}, f32[256,256]{1,0:T(8,128)}) fusion(f32[256,256]{1,0:T(8,128)S(1)} %collective-permute-done.1, bf16[16,128,2048]{1,2,0:T(8,128)(2,1)} %convert_bitcast_fusion, bf16[16,128,2048]{1,2,0:T(8,128)(2,1)S(1)} %bitcast_multiply_fusion), kind=kOutput, calls=%fused_computation.30 | convolution fusion | flops 268632064 | bytes 2752512 | tf_op jit(solution)/shard_map/kbi,kbj->ij/dot_general | solution.py:28
  48.1 1.1 stack.2
  49.1 6.8 %all-to-all-start = ((bf16[8,256,256]{2,1,0:T(8,128)(2,1)}), bf16[8,256,256]{2,1,0:T(8,128)(2,1)S(1)}, u32[]{:S(2)}, u32[]{:S(2)}) async-start(bf16[8,256,256]{2,1,0:T(8,128)(2,1)} %stack.2), calls=%async_computation | async-start | bytes 2097152 | tf_op jit(solution)/shard_map/all_to_all | solution.py:67
  56.0 0.0 copy-done.2
  56.0 0.1 copy.20
  56.1 44.0 %all-to-all-done = bf16[8,256,256]{2,1,0:T(8,128)(2,1)S(1)} async-done(((bf16[8,256,256]{2,1,0:T(8,128)(2,1)}), bf16[8,256,256]{2,1,0:T(8,128)(2,1)S(1)}, u32[]{:S(2)}, u32[]{:S(2)}) %all-to-all-start) | async-done | bytes 1048608 | tf_op jit(solution)/shard_map/all_to_all | solution.py:67
  100.1 1.2 %fusion.21 = f32[1,1,128,128]{3,2,1,0:T(8,128)} fusion(bf16[8,256,256]{2,1,0:T(8,128)(2,1)S(1)} %all-to-all-done, bf16[128,8,256]{2,1,0:T(8,128)(2,1)S(1)} %bitcast.53), kind=kOutput, calls=%fused_computation.20 | convolution fusion | flops 201588736 | bytes 1638400 | tf_op jit(solution)/shard_map/rnl,snl->rs/dot_general | solution.py:74
  101.2 0.0 collective-permute-done
  101.2 7.6 %fusion.7 = f32[1,1,768,768]{3,2,1,0:T(8,128)} fusion(f32[768,768]{1,0:T(8,128)} %collective-permute-done, bf16[16,128,2048]{1,2,0:T(8,128)(2,1)} %convert_bitcast_fusion, bf16[16,128,2048]{1,2,0:T(8,128)(2,1)} %copy-done.1), kind=kOutput, calls=%fused_computation.11 | convolution fusion | flops 2417098752 | bytes 11010048 | tf_op jit(solution)/shard_map/kbi,kbj->ij/dot_general | solution.py:28
  (1 shorter events, 0.0 us)
Async XLA Ops:
  0.6 19.6 %copy-start = (bf16[1,1,16,128,128]{4,3,2,1,0:T(8,128)(2,1)S(1)}, bf16[1,1,16,128,128]{4,3,2,1,0:T(8,128)(2,1)}, u32[]{:S(2)}) copy-start(bf16[1,1,16,128,128]{4,3,2,1,0:T(8,128)(2,1)} %param.6) | copy-start | bytes 1572868
  0.6 13.1 %copy-start.3 = (s32[1,1,16,16]{3,2,1,0:T(8,128)S(1)}, s32[1,1,16,16]{3,2,1,0:T(8,128)}, u32[]{:S(2)}) copy-start(s32[1,1,16,16]{3,2,1,0:T(8,128)} %param.7) | copy-start | bytes 3076
  20.3 25.4 %copy-start.1 = (bf16[16,128,2048]{1,2,0:T(8,128)(2,1)}, bf16[16,128,2048]{1,2,0:T(8,128)(2,1)S(1)}, u32[]{:S(2)}) copy-start(bf16[16,128,2048]{1,2,0:T(8,128)(2,1)S(1)} %bitcast_multiply_fusion) | copy-start | bytes 25165828
  27.3 28.6 %copy-start.2 = (bf16[1,1,128,2048]{3,2,1,0:T(8,128)(2,1)S(1)}, bf16[1,1,128,2048]{3,2,1,0:T(8,128)(2,1)}, u32[]{:S(2)}) copy-start(bf16[1,1,128,2048]{3,2,1,0:T(8,128)(2,1)} %param.9) | copy-start | bytes 1572868
  27.3 18.3 %collective-permute-start.1 = (f32[256,256]{1,0:T(8,128)S(1)}, f32[256,256]{1,0:T(8,128)S(1)}, u32[]{:S(2)}, u32[]{:S(2)}) collective-permute-start(f32[256,256]{1,0:T(8,128)S(1)} %fusion.18), channel_id=1, source_target_pairs={{0,32},{32,64},{64,96},{96,128},{128,160},{160,192},{192,224},{1,3... | collective-permute-start | bytes 786440 | tf_op jit(solution)/shard_map/ppermute | solution.py:14
  42.2 59.0 %collective-permute-start = (f32[768,768]{1,0:T(8,128)}, f32[768,768]{1,0:T(8,128)}, u32[]{:S(2)}, u32[]{:S(2)}) collective-permute-start(f32[768,768]{1,0:T(8,128)} %bitcast_negate_fusion), channel_id=1, source_target_pairs={{0,1},{1,2},{2,3},{3,4},{4,5},{5,6},{6,7},{7,8},{8,9},{9,10},{10,1... | collective-permute-start | bytes 7077896 | tf_op jit(solution)/shard_map/ppermute | solution.py:14
  49.1 50.9 %all-to-all-start = ((bf16[8,256,256]{2,1,0:T(8,128)(2,1)}), bf16[8,256,256]{2,1,0:T(8,128)(2,1)S(1)}, u32[]{:S(2)}, u32[]{:S(2)}) async-start(bf16[8,256,256]{2,1,0:T(8,128)(2,1)} %stack.2), calls=%async_computation | async-start | bytes 2097152 | tf_op jit(solution)/shard_map/all_to_all | solution.py:67
